TPU v7x, 32 devices: a whole 2x2x4 slice. The times are simulated.
32 devices in a mesh: fsdp: 8 (over y, x, core), dp: 4 (over z).
Axes of the slice: x: 2, y: 2, z: 4, core: 2. Of those that a mesh axis runs over, the one named last changes fastest.
Arguments:
- tokens: bfloat16 [16384, 768], P(('fsdp', 'dp')), may hold values from -6 to 6
- segment_ids: int32 [128, 128], P(('fsdp', 'dp')), may hold values from 0 to 7, never falling along the last dimension, each value on 1 to 32 neighbouring positions
- cotangent: bfloat16 [16384, 768], P(('fsdp', 'dp')), may hold values from -6 to 6
- qkv_weight: float32 [2, 768, 2304], P(None, 'fsdp'), may hold values from -0.21875 to 0.21875
- out_weight: float32 [2, 768, 768], P(None, 'fsdp'), may hold values from -0.875 to 0.875
- in_weight: float32 [2, 768, 3072], P(None, 'fsdp'), may hold values from -0.21875 to 0.21875
- back_weight: float32 [2, 3072, 768], P(None, 'fsdp'), may hold values from -0.109375 to 0.109375
- vectors: float32 [2, 12, 768], P(None, None, 'fsdp'), may hold values from -0.5 to 1.4, as said below
- qkv_moments: float32 [2, 2, 768, 2304], P(None, None, 'fsdp'), as said below
- out_moments: float32 [2, 2, 768, 768], P(None, None, 'fsdp'), as said below
- in_moments: float32 [2, 2, 768, 3072], P(None, None, 'fsdp'), as said below
- back_moments: float32 [2, 2, 3072, 768], P(None, None, 'fsdp'), as said below
- vector_moments: float32 [2, 2, 12, 768], P(None, None, None, 'fsdp'), as said below
Outputs:
- activations: bfloat16 [16384, 768], P(('fsdp', 'dp'))
- input_grad: float32 [16384, 768], P(('fsdp', 'dp'))
- qkv_grad: float32 [2, 768, 2304], P(None, 'fsdp')
- out_grad: float32 [2, 768, 768], P(None, 'fsdp')
- in_grad: float32 [2, 768, 3072], P(None, 'fsdp')
- back_grad: float32 [2, 3072, 768], P(None, 'fsdp')
- vector_grad: float32 [2, 12, 768], P(None, None, 'fsdp')
- qkv_new: float32 [2, 768, 2304], P(None, 'fsdp')
- out_new: float32 [2, 768, 768], P(None, 'fsdp')
- in_new: float32 [2, 768, 3072], P(None, 'fsdp')
- back_new: float32 [2, 3072, 768], P(None, 'fsdp')
- vector_new: float32 [2, 12, 768], P(None, None, 'fsdp')
- qkv_state: float32 [2, 768, 2304], P(None, 'fsdp')
- out_state: float32 [2, 768, 768], P(None, 'fsdp')
- in_state: float32 [2, 768, 3072], P(None, 'fsdp')
- back_state: float32 [2, 3072, 768], P(None, 'fsdp')
- vector_state: float32 [2, 12, 768], P(None, None, 'fsdp')
Inputs may be any that keep to these rules, and one draw needn't show every extreme that they name: `segment_ids`: within each packed row the numbers never fall and take every value 0 to 7, one per sentence; each sentence has 1 to 32 tokens and one has exactly 32. `vectors`: rows 3 and 10 of each layer are norm gains between 0.6 and 1.4; the other rows are biases between -0.5 and 0.5. `qkv_moments`: index 1 holds second moments, all positive. `out_moments`: index 1 holds second moments, all positive. `in_moments`: index 1 holds second moments, all positive. `back_moments`: index 1 holds second moments, all positive. `vector_moments`: index 1 holds second moments, all positive.
All inputs are finite; a program needn't handle non-finite values.
Results may differ from a plain program's by a relative error of at most 0.02.
Values may be sent and summed in bfloat16 or wider, within the bound.
A program may use at most 256 MiB of HBM per device.

v0:
```python
import jax
import jax.numpy as jnp
from jax import lax
from jax.sharding import PartitionSpec as P

HEADS = 12
HEAD_DIM = 64
LAYERS = 2
STEP = 3


EPSILON = 1e-05
NEGATIVE = -1000000000.0
BETA_FIRST = 0.5
BETA_SECOND = 0.5
WEIGHT_DECAY = 0.01
ADAM_EPSILON = 1e-08
RATE_MATRIX = 0.06
RATE_VECTOR = 0.5


def norm_forward(values, gain_row, shift_row):
    centered = values - jnp.mean(values, axis=-1, keepdims=True)
    inverse = lax.rsqrt(jnp.mean(centered * centered, axis=-1, keepdims=True) + EPSILON)
    scaled = centered * inverse
    return (scaled * gain_row + shift_row, scaled, inverse)


def norm_backward(grad_out, scaled, inverse, gain_row):
    grad_scaled = grad_out * gain_row
    grad_in = inverse * (
        grad_scaled
        - jnp.mean(grad_scaled, axis=-1, keepdims=True)
        - scaled * jnp.mean(grad_scaled * scaled, axis=-1, keepdims=True)
    )
    return (grad_in, jnp.sum(grad_out * scaled, axis=0), jnp.sum(grad_out, axis=0))


def score_block(queries, key_rows, same_segment):
    scores = jnp.einsum(
        "rqhe,rkhe->rhqk", queries, key_rows, preferred_element_type=jnp.float32
    ) * HEAD_DIM ** (-0.5)
    return jnp.where(same_segment, scores, NEGATIVE)


def layer_forward(hidden, same_segment, weights):
    qkv_used, out_used, in_used, back_used, vector_low = weights
    vector = vector_low.astype(jnp.float32)
    row_count = same_segment.shape[0]
    model_width = out_used.shape[0]
    hidden_low = hidden.astype(jnp.bfloat16)
    bias_qkv = jnp.concatenate([vector[0], jnp.zeros_like(vector[0]), vector[1]])
    joined = (jnp.dot(hidden_low, qkv_used, preferred_element_type=jnp.float32) + bias_qkv).astype(
        jnp.bfloat16
    )
    split_qkv = joined.reshape(row_count, -1, 3, HEADS, HEAD_DIM)
    scores = score_block(split_qkv[:, :, 0], split_qkv[:, :, 1], same_segment)
    row_top = jnp.max(scores, axis=-1, keepdims=True)
    log_total = row_top + jnp.log(jnp.sum(jnp.exp(scores - row_top), axis=-1, keepdims=True))
    prob_low = jnp.exp(scores - log_total).astype(jnp.bfloat16)
    attended = jnp.einsum(
        "rhqk,rkhe->rqhe", prob_low, split_qkv[:, :, 2], preferred_element_type=jnp.float32
    )
    attended_low = attended.reshape(-1, model_width).astype(jnp.bfloat16)
    branch = jnp.dot(attended_low, out_used, preferred_element_type=jnp.float32) + vector[2]
    first_norm, scaled_one, inverse_one = norm_forward(hidden + branch, vector[3], vector[4])
    first_low = first_norm.astype(jnp.bfloat16)
    inner_pre = jnp.dot(first_low, in_used, preferred_element_type=jnp.float32) + vector[
        5:9
    ].reshape(-1)
    active_low = jax.nn.gelu(inner_pre, approximate=False).astype(jnp.bfloat16)
    outer_out = jnp.dot(active_low, back_used, preferred_element_type=jnp.float32) + vector[9]
    output, scaled_two, inverse_two = norm_forward(first_norm + outer_out, vector[10], vector[11])
    kept_state = (
        hidden_low,
        joined,
        log_total,
        attended_low,
        scaled_one,
        inverse_one,
        first_low,
        inner_pre,
        active_low,
        scaled_two,
        inverse_two,
    )
    return (output, kept_state)


def layer_backward(grad_out, same_segment, weights, kept_state):
    qkv_used, out_used, in_used, back_used, vector_low = weights
    vector = vector_low.astype(jnp.float32)
    (
        hidden_low,
        joined,
        log_total,
        attended_low,
        scaled_one,
        inverse_one,
        first_low,
        inner_pre,
        active_low,
        scaled_two,
        inverse_two,
    ) = kept_state
    row_count = same_segment.shape[0]
    model_width = out_used.shape[0]
    grad_two, gain_two_grad, shift_two_grad = norm_backward(
        grad_out, scaled_two, inverse_two, vector[10]
    )
    grad_outer = grad_two.astype(jnp.bfloat16)
    back_bias_grad = jnp.sum(grad_two, axis=0)
    back_weight_grad = jnp.einsum(
        "tf,td->fd", active_low, grad_outer, preferred_element_type=jnp.float32
    )
    grad_active = jnp.einsum("td,fd->tf", grad_outer, back_used, preferred_element_type=jnp.float32)
    gelu_value, gelu_pull = jax.vjp(
        lambda values: jax.nn.gelu(values, approximate=False), inner_pre
    )
    grad_inner = gelu_pull(grad_active)[0].astype(jnp.bfloat16)
    in_bias_grad = jnp.sum(grad_inner, axis=0, dtype=jnp.float32)
    in_weight_grad = jnp.einsum(
        "td,tf->df", first_low, grad_inner, preferred_element_type=jnp.float32
    )
    grad_first = grad_two + jnp.einsum(
        "tf,df->td", grad_inner, in_used, preferred_element_type=jnp.float32
    )
    grad_one, gain_one_grad, shift_one_grad = norm_backward(
        grad_first, scaled_one, inverse_one, vector[3]
    )
    grad_branch = grad_one.astype(jnp.bfloat16)
    out_bias_grad = jnp.sum(grad_one, axis=0)
    out_weight_grad = jnp.einsum(
        "td,te->de", attended_low, grad_branch, preferred_element_type=jnp.float32
    )
    grad_mixed = jnp.einsum("te,de->td", grad_branch, out_used, preferred_element_type=jnp.float32)
    grad_mixed = grad_mixed.astype(jnp.bfloat16).reshape(row_count, -1, HEADS, HEAD_DIM)
    split_qkv = joined.reshape(row_count, -1, 3, HEADS, HEAD_DIM)
    queries = split_qkv[:, :, 0]
    key_rows = split_qkv[:, :, 1]
    value_rows = split_qkv[:, :, 2]
    prob_full = jnp.exp(score_block(queries, key_rows, same_segment) - log_total)
    prob_low = prob_full.astype(jnp.bfloat16)
    grad_values = jnp.einsum(
        "rhqk,rqhe->rkhe", prob_low, grad_mixed, preferred_element_type=jnp.float32
    )
    grad_probs = jnp.einsum(
        "rqhe,rkhe->rhqk", grad_mixed, value_rows, preferred_element_type=jnp.float32
    )
    centred = jnp.sum(prob_full * grad_probs, axis=-1, keepdims=True)
    grad_scores = (prob_full * (grad_probs - centred)).astype(jnp.bfloat16)
    grad_queries = jnp.einsum(
        "rhqk,rkhe->rqhe", grad_scores, key_rows, preferred_element_type=jnp.float32
    ) * HEAD_DIM ** (-0.5)
    grad_keys = jnp.einsum(
        "rhqk,rqhe->rkhe", grad_scores, queries, preferred_element_type=jnp.float32
    ) * HEAD_DIM ** (-0.5)
    grad_joined = (
        jnp.stack([grad_queries, grad_keys, grad_values], axis=2)
        .reshape(-1, 3 * model_width)
        .astype(jnp.bfloat16)
    )
    qkv_bias_grad = jnp.sum(grad_joined, axis=0, dtype=jnp.float32)
    qkv_weight_grad = jnp.einsum(
        "td,tc->dc", hidden_low, grad_joined, preferred_element_type=jnp.float32
    )
    grad_hidden = grad_one + jnp.einsum(
        "tc,dc->td", grad_joined, qkv_used, preferred_element_type=jnp.float32
    )
    vector_grad = jnp.concatenate(
        [
            qkv_bias_grad[:model_width][None],
            qkv_bias_grad[2 * model_width :][None],
            out_bias_grad[None],
            gain_one_grad[None],
            shift_one_grad[None],
            in_bias_grad.reshape(4, model_width),
            back_bias_grad[None],
            gain_two_grad[None],
            shift_two_grad[None],
        ],
        axis=0,
    )
    return (
        grad_hidden,
        (qkv_weight_grad, out_weight_grad, in_weight_grad, back_weight_grad, vector_grad),
    )


def adam_step(weight, gradient, moment_one, moment_two, step_rate):
    first_moment = BETA_FIRST * moment_one + (1.0 - BETA_FIRST) * gradient
    second_moment = BETA_SECOND * moment_two + (1.0 - BETA_SECOND) * gradient * gradient
    first_hat = first_moment / (1.0 - BETA_FIRST**STEP)
    second_hat = second_moment / (1.0 - BETA_SECOND**STEP)
    updated = weight - step_rate * (
        first_hat / (jnp.sqrt(second_hat) + ADAM_EPSILON) + WEIGHT_DECAY * weight
    )
    return jnp.stack([gradient, updated, second_moment])


def update_layer(summed, masters, moments, layer_at):
    outcome = []
    for kind_at in range(5):
        step_rate = RATE_VECTOR if kind_at == 4 else RATE_MATRIX
        outcome.append(
            adam_step(
                masters[kind_at][layer_at],
                summed[kind_at],
                moments[kind_at][0, layer_at],
                moments[kind_at][1, layer_at],
                step_rate,
            )
        )
    return outcome


def local_parts(masters, layer_at):
    return tuple((master[layer_at].astype(jnp.bfloat16) for master in masters))


def collect(results, kind_at, member):
    return jnp.stack([layer_result[kind_at][member] for layer_result in results])


def on_device(
    tokens,
    segment_ids,
    cotangent,
    qkv_weight,
    out_weight,
    in_weight,
    back_weight,
    vectors,
    qkv_moments,
    out_moments,
    in_moments,
    back_moments,
    vector_moments,
):
    masters = (qkv_weight, out_weight, in_weight, back_weight, vectors)
    moments = (qkv_moments, out_moments, in_moments, back_moments, vector_moments)
    same_segment = (segment_ids[:, :, None] == segment_ids[:, None, :])[:, None]
    hidden = tokens.astype(jnp.float32)
    saved_states = []
    for layer_at in range(LAYERS):
        parts_now = local_parts(masters, layer_at)
        weights = (
            lax.all_gather(parts_now[0], "fsdp", axis=0, tiled=True),
            lax.all_gather(parts_now[1], "fsdp", axis=0, tiled=True),
            lax.all_gather(parts_now[2], "fsdp", axis=0, tiled=True),
            lax.all_gather(parts_now[3], "fsdp", axis=0, tiled=True),
            lax.all_gather(parts_now[4], "fsdp", axis=1, tiled=True),
        )
        hidden, kept_state = layer_forward(hidden, same_segment, weights)
        saved_states.append(kept_state)
    activations = hidden.astype(jnp.bfloat16)
    grad_hidden = cotangent.astype(jnp.float32)
    results = [None] * LAYERS
    for layer_at in reversed(range(LAYERS)):
        parts_now = local_parts(masters, layer_at)
        weights = (
            lax.all_gather(parts_now[0], "fsdp", axis=0, tiled=True),
            lax.all_gather(parts_now[1], "fsdp", axis=0, tiled=True),
            lax.all_gather(parts_now[2], "fsdp", axis=0, tiled=True),
            lax.all_gather(parts_now[3], "fsdp", axis=0, tiled=True),
            lax.all_gather(parts_now[4], "fsdp", axis=1, tiled=True),
        )
        grad_hidden, weight_grads = layer_backward(
            grad_hidden, same_segment, weights, saved_states[layer_at]
        )
        shards = (
            lax.psum_scatter(
                weight_grads[0].astype(jnp.bfloat16), "fsdp", scatter_dimension=0, tiled=True
            ).astype(jnp.float32),
            lax.psum_scatter(
                weight_grads[1].astype(jnp.bfloat16), "fsdp", scatter_dimension=0, tiled=True
            ).astype(jnp.float32),
            lax.psum_scatter(
                weight_grads[2].astype(jnp.bfloat16), "fsdp", scatter_dimension=0, tiled=True
            ).astype(jnp.float32),
            lax.psum_scatter(
                weight_grads[3].astype(jnp.bfloat16), "fsdp", scatter_dimension=0, tiled=True
            ).astype(jnp.float32),
            lax.psum_scatter(
                weight_grads[4].astype(jnp.bfloat16), "fsdp", scatter_dimension=1, tiled=True
            ).astype(jnp.float32),
        )
        totals = (
            lax.psum(shards[0].astype(jnp.bfloat16), "dp").astype(jnp.float32),
            lax.psum(shards[1].astype(jnp.bfloat16), "dp").astype(jnp.float32),
            lax.psum(shards[2].astype(jnp.bfloat16), "dp").astype(jnp.float32),
            lax.psum(shards[3].astype(jnp.bfloat16), "dp").astype(jnp.float32),
            lax.psum(shards[4].astype(jnp.bfloat16), "dp").astype(jnp.float32),
        )
        results[layer_at] = update_layer(totals, masters, moments, layer_at)
    return (
        activations,
        grad_hidden,
        collect(results, 0, 0),
        collect(results, 1, 0),
        collect(results, 2, 0),
        collect(results, 3, 0),
        collect(results, 4, 0),
        collect(results, 0, 1),
        collect(results, 1, 1),
        collect(results, 2, 1),
        collect(results, 3, 1),
        collect(results, 4, 1),
        collect(results, 0, 2),
        collect(results, 1, 2),
        collect(results, 2, 2),
        collect(results, 3, 2),
        collect(results, 4, 2),
    )


def solution(mesh):
    in_specs = (
        P(("fsdp", "dp"), None),
        P(("fsdp", "dp"), None),
        P(("fsdp", "dp"), None),
        P(None, "fsdp", None),
        P(None, "fsdp", None),
        P(None, "fsdp", None),
        P(None, "fsdp", None),
        P(None, None, "fsdp"),
        P(None, None, "fsdp", None),
        P(None, None, "fsdp", None),
        P(None, None, "fsdp", None),
        P(None, None, "fsdp", None),
        P(None, None, None, "fsdp"),
    )
    out_specs = (
        P(("fsdp", "dp"), None),
        P(("fsdp", "dp"), None),
        P(None, "fsdp", None),
        P(None, "fsdp", None),
        P(None, "fsdp", None),
        P(None, "fsdp", None),
        P(None, None, "fsdp"),
        P(None, "fsdp", None),
        P(None, "fsdp", None),
        P(None, "fsdp", None),
        P(None, "fsdp", None),
        P(None, None, "fsdp"),
        P(None, "fsdp", None),
        P(None, "fsdp", None),
        P(None, "fsdp", None),
        P(None, "fsdp", None),
        P(None, None, "fsdp"),
    )
    return jax.shard_map(
        on_device, mesh=mesh, in_specs=in_specs, out_specs=out_specs, check_vma=False
    )
```

profile of v0, /device:TPU:0, one launch (start us, length us, event | category | flops | bytes accessed | tf_op | source)
XLA Modules:
  0.0 1014.2 jit_solution(5261636216384051771)
XLA Ops:
  18.0 10.5 %all-gather = bf16[8,96,12]{1,2,0:T(8,128)(2,1)S(1)} all-gather(bf16[1,96,12]{1,2,0:T(8,128)(2,1)S(1)} %bitcast.412), channel_id=1, replica_groups=mesh['fsdp'=8,'dp'=4] {'fsdp'}, dimensions={0}, use_global_device_ids=true | all-gather | bytes 20736 | tf_op jit(solution)/shard_map/all_gather | solution.py:252
  28.8 9.1 all-gather.1
  38.2 9.0 all-gather.11.cloned.1.call-done
  63.2 10.7 %all-gather.13.cloned.1.call-done = bf16[768,768]{1,0:T(8,128)(2,1)} async-done(((bf16[96,768]{1,0:T(8,128)(2,1)}), bf16[768,768]{1,0:T(8,128)(2,1)}) %all-gather.13.cloned.1.call-update) | async-done | bytes 1179664 | tf_op jit(solution)/shard_map/all_gather | solution.py:249
  76.4 38.9 %all-gather.15.cloned.1.call-done = bf16[768,3072]{1,0:T(8,128)(2,1)} async-done(((bf16[96,3072]{1,0:T(8,128)(2,1)}), bf16[768,3072]{1,0:T(8,128)(2,1)}) %all-gather.15.cloned.1.call-update) | async-done | bytes 4718608 | tf_op jit(solution)/shard_map/all_gather | solution.py:250
  115.2 19.7 %multiply_convert_fusion.1 = (bf16[512,3072]{1,0:T(8,128)(2,1)}, f32[512,3072]{1,0:T(8,128)}, f32[512,3072]{1,0:T(8,128)}) fusion(f32[3072]{0:T(1024)S(1)} %add.359, bf16[768,3072]{1,0:T(8,128)(2,1)} %all-gather.15.cloned.1.call-done, f32[512,768]{1,0:T(8,128)S(1)} %get-tuple-element.192, f32[768]{0:T(1024)S(1)} %get-tuple-element.111, ...), kind=kOutput, calls=%fused_computation.19 | convolution fusion | flops 2521694208 | bytes 22042624 | tf_op jit(solution)/shard_map/dot_general | solution.py:68
  135.0 21.5 %all-gather.17.cloned.1.call-done = bf16[3072,768]{1,0:T(8,128)(2,1)} async-done(((bf16[384,768]{1,0:T(8,128)(2,1)}), bf16[3072,768]{1,0:T(8,128)(2,1)}) %all-gather.17.cloned.1.call-update) | async-done | bytes 4718608 | tf_op jit(solution)/shard_map/all_gather | solution.py:251
  162.9 29.9 %all-gather.19.cloned.1.call-done = bf16[768,2304]{1,0:T(8,128)(2,1)} async-done(((bf16[96,2304]{1,0:T(8,128)(2,1)}), bf16[768,2304]{1,0:T(8,128)(2,1)}) %all-gather.19.cloned.1.call-update) | async-done | bytes 3538960 | tf_op jit(solution)/shard_map/all_gather | solution.py:248
  212.2 7.0 all-gather.21.cloned.1.call-done
  223.8 36.9 %all-gather.23.cloned.1.call-done = bf16[768,3072]{1,0:T(8,128)(2,1)} async-done(((bf16[96,3072]{1,0:T(8,128)(2,1)}), bf16[768,3072]{1,0:T(8,128)(2,1)}) %all-gather.23.cloned.1.call-update) | async-done | bytes 4718608 | tf_op jit(solution)/shard_map/all_gather | solution.py:250
  260.6 21.2 %multiply_convert_fusion = (bf16[512,3072]{1,0:T(8,128)(2,1)}, f32[512,3072]{1,0:T(8,128)}, f32[512,3072]{1,0:T(8,128)}) fusion(f32[3072]{0:T(1024)S(1)} %add.381, bf16[768,3072]{1,0:T(8,128)(2,1)} %all-gather.23.cloned.1.call-done, f32[512,768]{1,0:T(8,128)} %copy-done.12, f32[768]{0:T(1024)S(1)} %get-tuple-element.103, f32[768]{0:T(1024)S(1)} %get-tuple-element.104, ...), kind=kOutput, calls=%fused_computation.6 | convolution fusion | flops 2521694208 | bytes 22042624 | tf_op jit(solution)/shard_map/dot_general | solution.py:68
  281.8 20.2 %all-gather.25.cloned.1.call-done = bf16[3072,768]{1,0:T(8,128)(2,1)} async-done(((bf16[384,768]{1,0:T(8,128)(2,1)}), bf16[3072,768]{1,0:T(8,128)(2,1)}) %all-gather.25.cloned.1.call-update) | async-done | bytes 4718608 | tf_op jit(solution)/shard_map/all_gather | solution.py:251
  312.4 9.9 fusion.210
  358.3 10.1 fusion.211
  448.4 36.5 %reduce-scatter.31.cloned.1.call-done = bf16[96,2304]{1,0:T(8,128)(2,1)} async-done(((bf16[768,2304]{1,0:T(8,128)(2,1)}), bf16[96,2304]{1,0:T(8,128)(2,1)}) %reduce-scatter.31.cloned.1.call-update) | async-done | bytes 442384 | tf_op jit(solution)/shard_map/reduce_scatter | solution.py:272
  484.9 51.4 %reduce-scatter.33.cloned.1.call-done = bf16[96,2304]{1,0:T(8,128)(2,1)} async-done(((bf16[768,2304]{1,0:T(8,128)(2,1)}), bf16[96,2304]{1,0:T(8,128)(2,1)}) %reduce-scatter.33.cloned.1.call-update) | async-done | bytes 442384 | tf_op jit(solution)/shard_map/reduce_scatter | solution.py:272
  536.4 57.3 %reduce-scatter.29.cloned.1.call-done = bf16[384,768]{1,0:T(8,128)(2,1)} async-done(((bf16[3072,768]{1,0:T(8,128)(2,1)}), bf16[384,768]{1,0:T(8,128)(2,1)}) %reduce-scatter.29.cloned.1.call-update) | async-done | bytes 589840 | tf_op jit(solution)/shard_map/reduce_scatter | solution.py:281
  593.7 57.7 %reduce-scatter.23.cloned.1.call-done = bf16[96,3072]{1,0:T(8,128)(2,1)} async-done(((bf16[768,3072]{1,0:T(8,128)(2,1)}), bf16[96,3072]{1,0:T(8,128)(2,1)}) %reduce-scatter.23.cloned.1.call-update) | async-done | bytes 589840 | tf_op jit(solution)/shard_map/reduce_scatter | solution.py:278
  651.4 57.2 %reduce-scatter.25.cloned.1.call-done = bf16[96,3072]{1,0:T(8,128)(2,1)} async-done(((bf16[768,3072]{1,0:T(8,128)(2,1)}), bf16[96,3072]{1,0:T(8,128)(2,1)}) %reduce-scatter.25.cloned.1.call-update) | async-done | bytes 589840 | tf_op jit(solution)/shard_map/reduce_scatter | solution.py:278
  708.5 57.6 %reduce-scatter.27.cloned.1.call-done = bf16[384,768]{1,0:T(8,128)(2,1)} async-done(((bf16[3072,768]{1,0:T(8,128)(2,1)}), bf16[384,768]{1,0:T(8,128)(2,1)}) %reduce-scatter.27.cloned.1.call-update) | async-done | bytes 589840 | tf_op jit(solution)/shard_map/reduce_scatter | solution.py:281
  772.2 31.0 %reduce-scatter.35.cloned.1.call-done = bf16[96,12]{1,0:T(8,128)(2,1)} async-done(((bf16[768,12]{1,0:T(8,128)(2,1)}), bf16[96,12]{1,0:T(8,128)(2,1)}) %reduce-scatter.35.cloned.1.call-update) | async-done | bytes 2320
  804.0 36.5 %reduce-scatter.37.cloned.1.call-done = bf16[96,12]{1,0:T(8,128)(2,1)} async-done(((bf16[768,12]{1,0:T(8,128)(2,1)}), bf16[96,12]{1,0:T(8,128)(2,1)}) %reduce-scatter.37.cloned.1.call-update) | async-done | bytes 2320
  841.3 12.2 %all-reduce = (bf16[12,96]{1,0:T(8,128)(2,1)S(1)}, bf16[12,96]{1,0:T(8,128)(2,1)S(1)}) all-reduce(bf16[12,96]{1,0:T(8,128)(2,1)S(1)} %copy.209, bf16[12,96]{1,0:T(8,128)(2,1)S(1)} %copy.207), channel_id=1, replica_groups=mesh['fsdp'=8,'dp'=4] {'dp'}, use_global_device_ids=true, to_apply=%region_57.58 | all-reduce | flops 2304 | bytes 9216 | tf_op jit(solution)/shard_map/psum | solution.py:293
  855.4 124.4 %all-reduce.4.cloned.1.call-done = (bf16[96,2304]{1,0:T(8,128)(2,1)}, bf16[96,2304]{1,0:T(8,128)(2,1)}, bf16[96,768]{1,0:T(8,128)(2,1)}, bf16[96,768]{1,0:T(8,12...) async-done(((bf16[96,2304]{1,0:T(8,128)(2,1)}, bf16[96,2304]{1,0:T(8,128)(2,1)}, ...) | async-done | bytes 3538960 | tf_op jit(solution)/shard_map/psum | solution.py:289
  (425 shorter events, 221.9 us)
Async XLA Ops:
  7.2 40.1 %all-gather.11.cloned.1.call-start = ((), (), s32[]{:S(2)}) async-start(), calls=%async_computation.10 | async-start | bytes 3981312 | tf_op jit(solution)/shard_map/all_gather | solution.py:248
  9.8 64.1 %all-gather.13.cloned.1.call-start = ((), (), s32[]{:S(2)}) async-start(), calls=%async_computation.11 | async-start | bytes 1327104 | tf_op jit(solution)/shard_map/all_gather | solution.py:249
  10.6 104.7 %all-gather.15.cloned.1.call-start = ((), (), s32[]{:S(2)}) async-start(), calls=%async_computation.12 | async-start | bytes 5308416 | tf_op jit(solution)/shard_map/all_gather | solution.py:250
  13.5 143.0 %all-gather.17.cloned.1.call-start = ((), (), s32[]{:S(2)}) async-start(), calls=%async_computation.13 | async-start | bytes 5308416 | tf_op jit(solution)/shard_map/all_gather | solution.py:251
  14.7 178.1 %all-gather.19.cloned.1.call-start = ((), (), s32[]{:S(2)}) async-start(), calls=%async_computation.14 | async-start | bytes 3981312 | tf_op jit(solution)/shard_map/all_gather | solution.py:248
  15.3 203.9 %all-gather.21.cloned.1.call-start = ((), (), s32[]{:S(2)}) async-start(), calls=%async_computation.15 | async-start | bytes 1327104 | tf_op jit(solution)/shard_map/all_gather | solution.py:249
  15.9 244.8 %all-gather.23.cloned.1.call-start = ((), (), s32[]{:S(2)}) async-start(), calls=%async_computation.16 | async-start | bytes 5308416 | tf_op jit(solution)/shard_map/all_gather | solution.py:250
  16.6 285.4 %all-gather.25.cloned.1.call-start = ((), (), s32[]{:S(2)}) async-start(), calls=%async_computation.17 | async-start | bytes 5308416 | tf_op jit(solution)/shard_map/all_gather | solution.py:251
  17.3 431.0 %reduce-scatter.21.cloned.1.call-start = ((), (), s32[]{:S(2)}) async-start(), calls=%async_computation.19 | async-start | bytes 1327104 | tf_op jit(solution)/shard_map/reduce_scatter | solution.py:275
  28.7 326.9 %copy-start.73 = (f32[768]{0:T(1024)}, f32[768]{0:T(1024)S(1)}, u32[]{:S(2)}) copy-start(f32[768]{0:T(1024)S(1)} %get-tuple-element.108) | copy-start | bytes 9220
  28.7 343.3 %copy-start.69 = (f32[768]{0:T(1024)}, f32[768]{0:T(1024)S(1)}, u32[]{:S(2)}) copy-start(f32[768]{0:T(1024)S(1)} %get-tuple-element.112) | copy-start | bytes 9220
  76.4 295.7 %copy-start.76 = (f32[512]{0:T(512)}, f32[512]{0:T(512)S(1)}, u32[]{:S(2)}) copy-start(f32[512]{0:T(512)S(1)} %add_rsqrt_fusion.3) | copy-start | bytes 6148
  355.5 92.8 %reduce-scatter.19.cloned.1.call-start = ((), (), s32[]{:S(2)}) async-start(), calls=%async_computation.18 | async-start | bytes 1327104 | tf_op jit(solution)/shard_map/reduce_scatter | solution.py:275
  386.4 98.5 %reduce-scatter.31.cloned.1.call-start = ((), (), s32[]{:S(2)}) async-start(), calls=%async_computation.24 | async-start | bytes 3981312 | tf_op jit(solution)/shard_map/reduce_scatter | solution.py:272
  404.6 131.7 %reduce-scatter.33.cloned.1.call-start = ((), (), s32[]{:S(2)}) async-start(), calls=%async_computation.25 | async-start | bytes 3981312 | tf_op jit(solution)/shard_map/reduce_scatter | solution.py:272
  411.9 181.8 %reduce-scatter.29.cloned.1.call-start = ((), (), s32[]{:S(2)}) async-start(), calls=%async_computation.23 | async-start | bytes 5308416 | tf_op jit(solution)/shard_map/reduce_scatter | solution.py:281
  420.1 231.3 %reduce-scatter.23.cloned.1.call-start = ((), (), s32[]{:S(2)}) async-start(), calls=%async_computation.20 | async-start | bytes 5308416 | tf_op jit(solution)/shard_map/reduce_scatter | solution.py:278
  428.0 280.5 %reduce-scatter.25.cloned.1.call-start = ((), (), s32[]{:S(2)}) async-start(), calls=%async_computation.21 | async-start | bytes 5308416 | tf_op jit(solution)/shard_map/reduce_scatter | solution.py:278
  436.0 330.2 %reduce-scatter.27.cloned.1.call-start = ((), (), s32[]{:S(2)}) async-start(), calls=%async_computation.22 | async-start | bytes 5308416 | tf_op jit(solution)/shard_map/reduce_scatter | solution.py:281
  444.2 359.0 %reduce-scatter.35.cloned.1.call-start = ((), (), s32[]{:S(2)}) async-start(), calls=%async_computation.26 | async-start | bytes 221184
  445.4 320.8 %copy-start.64 = (f32[2,2,12,96]{3,1,2,0:T(2,128)S(1)}, f32[2,2,12,96]{3,1,2,0:T(2,128)}, u32[]{:S(2)}) copy-start(f32[2,2,12,96]{3,1,2,0:T(2,128)} %param.25) | copy-start | bytes 55300
  445.5 320.8 %copy-start.5 = (f32[512,768]{1,0:T(8,128)S(1)}, f32[512,768]{1,0:T(8,128)}, u32[]{:S(2)}) copy-start(f32[512,768]{1,0:T(8,128)} %copy-done.4) | copy-start | bytes 4718596
  446.9 393.7 %reduce-scatter.37.cloned.1.call-start = ((), (), s32[]{:S(2)}) async-start(), calls=%async_computation.27 | async-start | bytes 221184
  448.3 531.6 %all-reduce.4.cloned.1.call-start = ((), (), s32[]{:S(2)}) async-start(), calls=%async_computation.28 | async-start | bytes 7077888 | tf_op jit(solution)/shard_map/psum | solution.py:289
  (110 other events, 2320.1 us)
Sparse Core Ops, SparseCore 0:
  10.5 36.7 all-gather.10
  49.7 24.0 all-gather.12
  76.3 38.9 all-gather.14
  117.6 38.9 all-gather.16
  158.8 33.9 all-gather.18
  195.1 24.0 all-gather.20
  221.7 38.9 all-gather.22
  263.1 38.9 all-gather.24
  355.6 36.7 reduce-scatter.20
  396.5 36.7 reduce-scatter.18
  436.8 48.0 reduce-scatter.30
  488.2 48.0 reduce-scatter.32
  539.8 53.8 reduce-scatter.28
  597.4 53.9 reduce-scatter.22
  654.6 53.8 reduce-scatter.24
  712.2 53.8 reduce-scatter.26
  769.6 33.5 reduce-scatter.34
  806.9 33.5 reduce-scatter.36
  843.5 136.3 all-reduce.3
where the time goes:
time: 1020 us; the launch traced here: 1010 us
  waiting for transfers between devices  687 us (67%)
  matrix products  169 us (17%)
  local copies, waits for them, and re-layouts  68.4 us (7%)
  other arithmetic  41.6 us (4%)
  blocking collectives  31.8 us (3%)
  between operations  15.7 us (2%)
    psum x1, waiting for transfers between devices, on_device(): lax.psum(shards[0].astype(jnp.bfloat16), 'dp').astype(jnp.float32)  124 us
    reduce_scatter x2, waiting for transfers between devices, on_device(): lax.psum_scatter(weight_grads[3].astype(jnp.bfloat16), 'fsdp', scatter_di...  115 us
    reduce_scatter x2, waiting for transfers between devices, on_device(): lax.psum_scatter(weight_grads[2].astype(jnp.bfloat16), 'fsdp', scatter_di...  115 us
    reduce_scatter x2, waiting for transfers between devices, on_device(): lax.psum_scatter(weight_grads[0].astype(jnp.bfloat16), 'fsdp', scatter_di...  88 us
    all_gather x2, waiting for transfers between devices, on_device(): lax.all_gather(parts_now[2], 'fsdp', axis=0, tiled=True)  75.7 us
    unnamed x21, waiting for transfers between devices  70.2 us
    all_gather x2, waiting for transfers between devices, on_device(): lax.all_gather(parts_now[3], 'fsdp', axis=0, tiled=True)  41.7 us
    dot_general x2, matrix products, layer_forward(): jnp.dot(first_low, in_used, preferred_element_type=jnp.float32)  40.9 us
  transfers between devices with their start and end apart: 19, of which 17 were waited for; matrix products, arithmetic and copies ran while one was open for 18% of the time, Pallas kernels for 0%

commit v1 on v0

--- a/solution.py
+++ b/solution.py
@@ -1,13 +1,16 @@
 import jax
 import jax.numpy as jnp
 from jax import lax
+from jax.experimental import pallas as pl
+from jax.experimental.pallas import tpu as pltpu
 from jax.sharding import PartitionSpec as P
 
 HEADS = 12
 HEAD_DIM = 64
 LAYERS = 2
 STEP = 3
-
+ROW = 128
+LANES = 128
 
 EPSILON = 1e-05
 NEGATIVE = -1000000000.0
@@ -17,6 +20,419 @@
 ADAM_EPSILON = 1e-08
 RATE_MATRIX = 0.06
 RATE_VECTOR = 0.5
+MESH_ID = pl.DeviceIdType.MESH
+BF16 = jnp.bfloat16
+F32 = jnp.float32
+
+
+class Place:
+    def __init__(self):
+        f = lax.axis_index("fsdp")
+        z = lax.axis_index("dp")
+        core = lax.rem(f, 2)
+        x = lax.rem(lax.div(f, 2), 2)
+        y = lax.div(f, 4)
+        self.f, self.z, self.core, self.x, self.y = f, z, core, x, y
+        self.fc = f + 1 - 2 * core
+        self.fx = f + 2 - 4 * x
+        self.fy = f + 4 - 8 * y
+        self.fd = self.fx + 4 - 8 * y
+        self.q = lax.rem(z, 2)
+        self.to_c = {"fsdp": self.fc}
+        self.to_x = {"fsdp": self.fx}
+        self.to_y = {"fsdp": self.fy}
+        self.to_z = {"dp": z + 1 - 2 * self.q}
+
+
+def greet(partners):
+    barrier = pltpu.get_barrier_semaphore()
+    for partner in partners:
+        pl.semaphore_signal(barrier, inc=1, device_id=partner, device_id_type=MESH_ID)
+    pl.semaphore_wait(barrier, len(partners))
+
+
+def norm_rows(values, gain_row, shift_row):
+    centered = values - jnp.mean(values, axis=-1, keepdims=True)
+    inverse = lax.rsqrt(jnp.mean(centered * centered, axis=-1, keepdims=True) + EPSILON)
+    scaled = centered * inverse
+    return scaled * gain_row + shift_row, scaled, inverse
+
+
+def gelu_pair(value):
+    cdf = 0.5 * (1.0 + lax.erf(value * 0.7071067811865476))
+    slope = cdf + value * (0.3989422804014327 * jnp.exp(-0.5 * value * value))
+    return value * cdf, slope
+
+
+COPY_KINDS = 15
+VEC_KINDS = 7
+
+
+def forward_kernel(
+    tok_ref, seg_ref, vec_ref, own_q, own_o, own_i, own_b,
+    act_out, wq_out, wo_out, wi_out, wb_out, vec_out,
+    joined_out, att_out, xh1_out, r1_out, flow_out, active_out, slope_out, xh2_out, r2_out, hlow_out,
+    wq0, wo0, wi0, wb0, wq1, wo1, wi1, wb1, vslots, vec,
+    hid, hlow, joined, att, first, xh1, r1, flow, active, slope, xh2, r2, mask,
+    send_sem, recv_sem, own_sem, wout_sem, save_sem,
+):
+    here = Place()
+    owns = (own_q, own_o, own_i, own_b)
+    bufs = ((wq0, wo0, wi0, wb0), (wq1, wo1, wi1, wb1))
+    wouts = (wq_out, wo_out, wi_out, wb_out)
+    f, fx, fy, fd = here.f, here.fx, here.fy, here.fd
+    greet((here.to_c, here.to_x, here.to_y, here.to_z))
+
+    started = []
+
+    def make(p, kind):
+        layer, kind_at = divmod(p, 4)
+        own, buf = owns[kind_at].at[layer], bufs[layer][kind_at]
+        rows, cols = own.shape
+        third = cols // 3
+        c_xy = pl.multiple_of(here.q * third, LANES)
+        c_b = pl.multiple_of(c_xy + third, LANES)
+        c_z = pl.multiple_of(here.q * (2 * third), LANES)
+        c_w = pl.multiple_of((1 - here.q) * (2 * third), LANES)
+
+        def win(owner, col, width):
+            return buf.at[pl.ds(pl.multiple_of(owner * rows, 32), rows), pl.ds(col, width)]
+
+        two = 2 * third
+        table = {
+            0: (own, win(f, 0, cols), here.to_c),
+            1: (own.at[:, pl.ds(c_xy, two)], win(f, c_xy, two), here.to_x),
+            2: (own.at[:, pl.ds(c_xy, two)], win(f, c_xy, two), here.to_y),
+            3: (win(fx, c_xy, two), win(fx, c_xy, two), here.to_c),
+            4: (win(fx, c_xy, third), win(fx, c_xy, third), here.to_y),
+            5: (win(fx, c_z, third), win(fx, c_z, third), here.to_z),
+            6: (win(fy, c_xy, two), win(fy, c_xy, two), here.to_c),
+            7: (win(fy, c_b, third), win(fy, c_b, third), here.to_x),
+            8: (win(fy, c_z, third), win(fy, c_z, third), here.to_z),
+            9: (win(fd, c_xy, third), win(fd, c_xy, third), here.to_c),
+            10: (win(fd, c_b, third), win(fd, c_b, third), here.to_c),
+            11: (win(fd, c_z, third), win(fd, c_z, third), here.to_z),
+            12: (win(fx, c_w, third), win(fx, c_w, third), here.to_c),
+            13: (win(fy, c_w, third), win(fy, c_w, third), here.to_c),
+            14: (win(fd, c_w, third), win(fd, c_w, third), here.to_c),
+        }
+        src, dst, dev = table[kind]
+        slot = p * COPY_KINDS + kind
+        return pltpu.make_async_remote_copy(
+            src_ref=src, dst_ref=dst, send_sem=send_sem.at[slot], recv_sem=recv_sem.at[slot],
+            device_id=dev, device_id_type=MESH_ID,
+        )
+
+    copies = {}
+
+    def start(p, *kinds):
+        for kind in kinds:
+            copy = make(p, kind)
+            copy.start()
+            copies[p, kind] = copy
+            started.append(copy)
+
+    def arrived(p, *kinds):
+        for kind in kinds:
+            copies[p, kind].wait_recv()
+
+    def local_own(p):
+        layer, kind_at = divmod(p, 4)
+        own, buf = owns[kind_at].at[layer], bufs[layer][kind_at]
+        rows = own.shape[0]
+        return pltpu.make_async_copy(
+            own, buf.at[pl.ds(pl.multiple_of(f * rows, 32), rows)], own_sem.at[p]
+        )
+
+    def send_own(p):
+        if p < 8:
+            start(p, 1, 2, 0)
+            local_own(p).start()
+
+    def stage_one(p):
+        if p < 8:
+            arrived(p, 1, 2)
+            start(p, 4, 7, 5, 8, 3, 6)
+
+    def stage_two(p):
+        arrived(p, 4, 7)
+        start(p, 11, 9, 10)
+
+    def stage_three(p):
+        arrived(p, 5, 8, 11)
+        start(p, 12, 13, 14)
+
+    wcopies = []
+
+    def stage_four(p):
+        layer, kind_at = divmod(p, 4)
+        local_own(p).wait()
+        arrived(p, 0, 3, 6, 9, 10, 12, 13, 14)
+        copy = pltpu.make_async_copy(bufs[layer][kind_at], wouts[kind_at].at[layer], wout_sem.at[p])
+        copy.start()
+        wcopies.append(copy)
+
+    def advance(p):
+        stage_one(p + 1)
+        send_own(p + 3)
+        stage_two(p)
+        stage_three(p)
+        stage_four(p)
+
+    vslots[pl.ds(f, 1)] = vec_ref[...][None]
+
+    def vcopy(kind):
+        owner, dev = {
+            0: (f, here.to_x), 1: (f, here.to_y), 2: (f, here.to_c),
+            3: (fx, here.to_y), 4: (fx, here.to_c), 5: (fy, here.to_c), 6: (fd, here.to_c),
+        }[kind]
+        slot = 8 * COPY_KINDS + kind
+        return pltpu.make_async_remote_copy(
+            src_ref=vslots.at[owner], dst_ref=vslots.at[owner], send_sem=send_sem.at[slot],
+            recv_sem=recv_sem.at[slot], device_id=dev, device_id_type=MESH_ID,
+        )
+
+    vc = [vcopy(kind) for kind in range(VEC_KINDS)]
+    started.extend(vc)
+    for kind in (0, 1, 2):
+        vc[kind].start()
+    send_own(0)
+    send_own(1)
+    send_own(2)
+
+    rows_here = seg_ref.shape[0]
+    for r in range(rows_here):
+        wide = jnp.broadcast_to(seg_ref[r : r + 1, :].astype(F32), (ROW, ROW))
+        mask[r] = jnp.where(wide == wide.T, 1.0, 0.0)
+
+    vc[0].wait_recv()
+    vc[1].wait_recv()
+    for kind in (3, 4, 5):
+        vc[kind].start()
+    vc[3].wait_recv()
+    vc[6].start()
+    for kind in (2, 4, 5, 6):
+        vc[kind].wait_recv()
+    width = vec.shape[1]
+    share = width // 8
+    lane = lax.broadcasted_iota(jnp.int32, (LANES, width), 0)
+    column = lax.broadcasted_iota(jnp.int32, (LANES, width), 1)
+    whole = jnp.zeros(vec.shape, F32)
+    for owner in range(8):
+        pick = (column == lane + owner * share) & (lane < share)
+        whole = whole + jnp.dot(
+            vslots[owner], jnp.where(pick, 1.0, 0.0).astype(BF16), preferred_element_type=F32
+        )
+    vec[...] = whole
+
+    tokens = hid.shape[0]
+    saves = {}
+
+    def save(layer, at, src, dst):
+        copy = pltpu.make_async_copy(src, dst, save_sem.at[layer, at])
+        copy.start()
+        saves[layer, at] = copy
+
+    def saved(layer, *ats):
+        if layer >= 0:
+            for at in ats:
+                saves[layer, at].wait()
+
+    stage_one(0)
+    half = tokens // 2
+    for layer in range(LAYERS):
+        wq, wo, wi, wb = bufs[layer]
+        base = 12 * layer
+
+        def row(at):
+            return vec[base + at : base + at + 1, :]
+
+        low_ref = tok_ref if layer == 0 else hlow
+        advance(4 * layer)
+        saved(layer - 1, 0)
+        for part in range(3):
+            bias = row(0) if part == 0 else row(1)
+
+            def qkv_tile(n, carry, part=part, bias=bias):
+                at = pl.multiple_of(n * half, half)
+                acc = jnp.dot(
+                    low_ref[pl.ds(at, half), :], wq[:, part * width : (part + 1) * width],
+                    preferred_element_type=F32,
+                )
+                if part != 1:
+                    acc = acc + bias
+                joined[pl.ds(at, half), part * width : (part + 1) * width] = acc.astype(BF16)
+                return carry
+
+            lax.fori_loop(0, 2, qkv_tile, 0)
+        save(layer, 0, joined, joined_out.at[layer])
+        saved(layer - 1, 1)
+
+        def attend(step, carry):
+            r = lax.div(step, HEADS // 2)
+            j = lax.rem(step, HEADS // 2)
+            rows = pl.ds(pl.multiple_of(r * ROW, ROW), ROW)
+
+            def cols(part):
+                return pl.ds(pl.multiple_of(part * width + j * LANES, LANES), LANES)
+
+            query, keys, value = (joined[rows, cols(part)] for part in range(3))
+            first_head = lax.broadcasted_iota(jnp.int32, (ROW, LANES), 1) < HEAD_DIM
+            nil = jnp.zeros_like(query)
+            both = jnp.concatenate(
+                [jnp.where(first_head, query, nil), jnp.where(first_head, nil, query)], axis=0
+            )
+            scores = lax.dot_general(
+                both, keys, (((1,), (1,)), ((), ())), preferred_element_type=F32
+            ) * HEAD_DIM ** (-0.5)
+            seen = mask[pl.ds(r, 1)][0]
+            scores = jnp.where(jnp.concatenate([seen, seen], axis=0) > 0.5, scores, NEGATIVE)
+            top = jnp.max(scores, axis=-1, keepdims=True)
+            grown = jnp.exp(scores - top)
+            probs = grown / jnp.sum(grown, axis=-1, keepdims=True)
+            mixed = jnp.dot(probs.astype(BF16), value, preferred_element_type=F32)
+            att[rows, pl.ds(pl.multiple_of(j * LANES, LANES), LANES)] = jnp.where(
+                first_head, mixed[:ROW], mixed[ROW:]
+            ).astype(BF16)
+            return carry
+
+        lax.fori_loop(0, rows_here * (HEADS // 2), attend, 0)
+        save(layer, 1, att, att_out.at[layer])
+        advance(4 * layer + 1)
+        saved(layer - 1, 2, 3, 4)
+
+        def out_tile(n, carry):
+            rows = pl.ds(pl.multiple_of(n * ROW, ROW), ROW)
+            branch = jnp.dot(att[rows, :], wo[...], preferred_element_type=F32) + row(2)
+            before = tok_ref[rows, :].astype(F32) if layer == 0 else hid[rows, :]
+            normed, scaled, inverse = norm_rows(before + branch, row(3), row(4))
+            first[rows, :] = normed
+            flow[rows, :] = normed.astype(BF16)
+            xh1[rows, :] = scaled
+            r1[rows, :] = jnp.broadcast_to(inverse, (ROW, LANES))
+            return carry
+
+        lax.fori_loop(0, tokens // ROW, out_tile, 0)
+        save(layer, 2, xh1, xh1_out.at[layer])
+        save(layer, 3, r1, r1_out.at[layer])
+        save(layer, 4, flow, flow_out.at[layer])
+        advance(4 * layer + 2)
+        saved(layer - 1, 5, 6)
+        parts = wi.shape[1] // width
+        tile = 256
+        for part in range(parts):
+            bias_row = row(5 + part)
+            for sub in range(width // tile):
+                bias = bias_row[:, sub * tile : (sub + 1) * tile]
+                cols = slice(part * width + sub * tile, part * width + (sub + 1) * tile)
+
+                def in_tile(n, carry, cols=cols, bias=bias):
+                    rows = pl.ds(pl.multiple_of(n * half, half), half)
+                    inner = jnp.dot(flow[rows, :], wi[:, cols], preferred_element_type=F32) + bias
+                    value, change = gelu_pair(inner)
+                    active[rows, cols] = value.astype(BF16)
+                    slope[rows, cols] = change.astype(BF16)
+                    return carry
+
+                lax.fori_loop(0, 2, in_tile, 0)
+        save(layer, 5, active, active_out.at[layer])
+        save(layer, 6, slope, slope_out.at[layer])
+        advance(4 * layer + 3)
+        saved(layer - 1, 7, 8)
+
+        def back_tile(n, carry):
+            rows = pl.ds(pl.multiple_of(n * ROW, ROW), ROW)
+            outer = jnp.dot(active[rows, :], wb[...], preferred_element_type=F32) + row(9)
+            normed, scaled, inverse = norm_rows(first[rows, :] + outer, row(10), row(11))
+            xh2[rows, :] = scaled
+            r2[rows, :] = jnp.broadcast_to(inverse, (ROW, LANES))
+            if layer == LAYERS - 1:
+                act_out[rows, :] = normed.astype(BF16)
+            else:
+                hid[rows, :] = normed
+                hlow[rows, :] = normed.astype(BF16)
+            return carry
+
+        lax.fori_loop(0, tokens // ROW, back_tile, 0)
+        save(layer, 7, xh2, xh2_out.at[layer])
+        save(layer, 8, r2, r2_out.at[layer])
+        if layer == 0:
+            save(layer, 9, hlow, hlow_out)
+    vec_save = pltpu.make_async_copy(vec, vec_out, save_sem.at[1, 9])
+    vec_save.start()
+    for copy in started:
+        copy.wait_send()
+    for copy in wcopies:
+        copy.wait()
+    saved(0, 9)
+    saved(1, *range(9))
+    vec_save.wait()
+
+
+def forward(tokens, segment_ids, vec_low, qkv_low, out_low, in_low, back_low):
+    count, width = tokens.shape
+    ff = in_low.shape[2]
+    any_spec = pl.BlockSpec(memory_space=pltpu.HBM)
+    vmem = pl.BlockSpec(memory_space=pltpu.VMEM)
+
+    def shape(dims, kind):
+        return jax.ShapeDtypeStruct(dims, kind)
+
+    out_shape = (
+        shape((count, width), BF16),
+        shape((LAYERS, width, 3 * width), BF16),
+        shape((LAYERS, width, width), BF16),
+        shape((LAYERS, width, ff), BF16),
+        shape((LAYERS, ff, width), BF16),
+        shape((vec_low.shape[0], width), F32),
+        shape((LAYERS, count, 3 * width), BF16),
+        shape((LAYERS, count, width), BF16),
+        shape((LAYERS, count, width), F32),
+        shape((LAYERS, count, LANES), F32),
+        shape((LAYERS, count, width), BF16),
+        shape((LAYERS, count, ff), BF16),
+        shape((LAYERS, count, ff), BF16),
+        shape((LAYERS, count, width), F32),
+        shape((LAYERS, count, LANES), F32),
+        shape((count, width), BF16),
+    )
+    weights = [
+        pltpu.VMEM((width, 3 * width), BF16), pltpu.VMEM((width, width), BF16),
+        pltpu.VMEM((width, ff), BF16), pltpu.VMEM((ff, width), BF16),
+    ]
+    scratch = weights * LAYERS + [
+        pltpu.VMEM((8,) + vec_low.shape, BF16),
+        pltpu.VMEM((vec_low.shape[0], width), F32),
+        pltpu.VMEM((count, width), F32),
+        pltpu.VMEM((count, width), BF16),
+        pltpu.VMEM((count, 3 * width), BF16),
+        pltpu.VMEM((count, width), BF16),
+        pltpu.VMEM((count, width), F32),
+        pltpu.VMEM((count, width), F32),
+        pltpu.VMEM((count, LANES), F32),
+        pltpu.VMEM((count, width), BF16),
+        pltpu.VMEM((count, ff), BF16),
+        pltpu.VMEM((count, ff), BF16),
+        pltpu.VMEM((count, width), F32),
+        pltpu.VMEM((count, LANES), F32),
+        pltpu.VMEM((segment_ids.shape[0], ROW, ROW), F32),
+        pltpu.SemaphoreType.DMA((8 * COPY_KINDS + VEC_KINDS,)),
+        pltpu.SemaphoreType.DMA((8 * COPY_KINDS + VEC_KINDS,)),
+        pltpu.SemaphoreType.DMA((8,)),
+        pltpu.SemaphoreType.DMA((8,)),
+        pltpu.SemaphoreType.DMA((LAYERS, 10)),
+    ]
+    return pl.pallas_call(
+        forward_kernel,
+        name="forward",
+        out_shape=out_shape,
+        in_specs=[vmem, vmem, vmem] + [any_spec] * 4,
+        out_specs=[vmem] + [any_spec] * (len(out_shape) - 1),
+        scratch_shapes=scratch,
+        compiler_params=pltpu.CompilerParams(
+            collective_id=0, has_side_effects=True, vmem_limit_bytes=60 << 20
+        ),
+    )(tokens, segment_ids, vec_low, qkv_low, out_low, in_low, back_low)
 
 
 def norm_forward(values, gain_row, shift_row):
@@ -114,10 +530,13 @@
         "tf,td->fd", active_low, grad_outer, preferred_element_type=jnp.float32
     )
     grad_active = jnp.einsum("td,fd->tf", grad_outer, back_used, preferred_element_type=jnp.float32)
-    gelu_value, gelu_pull = jax.vjp(
-        lambda values: jax.nn.gelu(values, approximate=False), inner_pre
-    )
-    grad_inner = gelu_pull(grad_active)[0].astype(jnp.bfloat16)
+    if inner_pre.dtype == BF16:
+        grad_inner = (grad_active * inner_pre.astype(F32)).astype(BF16)
+    else:
+        gelu_value, gelu_pull = jax.vjp(
+            lambda values: jax.nn.gelu(values, approximate=False), inner_pre
+        )
+        grad_inner = gelu_pull(grad_active)[0].astype(jnp.bfloat16)
     in_bias_grad = jnp.sum(grad_inner, axis=0, dtype=jnp.float32)
     in_weight_grad = jnp.einsum(
         "td,tf->df", first_low, grad_inner, preferred_element_type=jnp.float32
@@ -222,7 +641,7 @@
     return jnp.stack([layer_result[kind_at][member] for layer_result in results])
 
 
-def on_device(
+def on_device_any(
     tokens,
     segment_ids,
     cotangent,
@@ -314,6 +733,101 @@
     )
 
 
+def split_heads(joined, rows):
+    return joined.reshape(rows, -1, 3, HEADS, HEAD_DIM)
+
+
+def on_device(
+    tokens,
+    segment_ids,
+    cotangent,
+    qkv_weight,
+    out_weight,
+    in_weight,
+    back_weight,
+    vectors,
+    qkv_moments,
+    out_moments,
+    in_moments,
+    back_moments,
+    vector_moments,
+):
+    masters = (qkv_weight, out_weight, in_weight, back_weight, vectors)
+    moments = (qkv_moments, out_moments, in_moments, back_moments, vector_moments)
+    same_segment = (segment_ids[:, :, None] == segment_ids[:, None, :])[:, None]
+    share = vectors.shape[2]
+    vec_low = jnp.pad(vectors.reshape(-1, share), ((0, 8), (0, LANES - share))).astype(BF16)
+    (
+        activations, wq, wo, wi, wb, vec,
+        joined, att, xh1, r1, flow, active, slope, xh2, r2, hlow,
+    ) = forward(
+        tokens, segment_ids, vec_low, qkv_weight.astype(BF16), out_weight.astype(BF16),
+        in_weight.astype(BF16), back_weight.astype(BF16),
+    )
+    grad_hidden = cotangent.astype(jnp.float32)
+    results = [None] * LAYERS
+    rows = segment_ids.shape[0]
+    for layer_at in reversed(range(LAYERS)):
+        split_qkv = split_heads(joined[layer_at], rows)
+        scores = score_block(split_qkv[:, :, 0], split_qkv[:, :, 1], same_segment)
+        row_top = jnp.max(scores, axis=-1, keepdims=True)
+        log_total = row_top + jnp.log(jnp.sum(jnp.exp(scores - row_top), axis=-1, keepdims=True))
+        kept = (
+            tokens if layer_at == 0 else hlow, joined[layer_at], log_total, att[layer_at],
+            xh1[layer_at], r1[layer_at][:, :1], flow[layer_at], slope[layer_at], active[layer_at],
+            xh2[layer_at], r2[layer_at][:, :1],
+        )
+        weights = (
+            wq[layer_at], wo[layer_at], wi[layer_at], wb[layer_at],
+            vec[12 * layer_at : 12 * layer_at + 12],
+        )
+        grad_hidden, weight_grads = layer_backward(grad_hidden, same_segment, weights, kept)
+        shards = (
+            lax.psum_scatter(
+                weight_grads[0].astype(jnp.bfloat16), "fsdp", scatter_dimension=0, tiled=True
+            ).astype(jnp.float32),
+            lax.psum_scatter(
+                weight_grads[1].astype(jnp.bfloat16), "fsdp", scatter_dimension=0, tiled=True
+            ).astype(jnp.float32),
+            lax.psum_scatter(
+                weight_grads[2].astype(jnp.bfloat16), "fsdp", scatter_dimension=0, tiled=True
+            ).astype(jnp.float32),
+            lax.psum_scatter(
+                weight_grads[3].astype(jnp.bfloat16), "fsdp", scatter_dimension=0, tiled=True
+            ).astype(jnp.float32),
+            lax.psum_scatter(
+                weight_grads[4].astype(jnp.bfloat16), "fsdp", scatter_dimension=1, tiled=True
+            ).astype(jnp.float32),
+        )
+        totals = (
+            lax.psum(shards[0].astype(jnp.bfloat16), "dp").astype(jnp.float32),
+            lax.psum(shards[1].astype(jnp.bfloat16), "dp").astype(jnp.float32),
+            lax.psum(shards[2].astype(jnp.bfloat16), "dp").astype(jnp.float32),
+            lax.psum(shards[3].astype(jnp.bfloat16), "dp").astype(jnp.float32),
+            lax.psum(shards[4].astype(jnp.bfloat16), "dp").astype(jnp.float32),
+        )
+        results[layer_at] = update_layer(totals, masters, moments, layer_at)
+    return (
+        activations,
+        grad_hidden,
+        collect(results, 0, 0),
+        collect(results, 1, 0),
+        collect(results, 2, 0),
+        collect(results, 3, 0),
+        collect(results, 4, 0),
+        collect(results, 0, 1),
+        collect(results, 1, 1),
+        collect(results, 2, 1),
+        collect(results, 3, 1),
+        collect(results, 4, 1),
+        collect(results, 0, 2),
+        collect(results, 1, 2),
+        collect(results, 2, 2),
+        collect(results, 3, 2),
+        collect(results, 4, 2),
+    )
+
+
 def solution(mesh):
     in_specs = (
         P(("fsdp", "dp"), None),
@@ -349,6 +863,7 @@
         P(None, "fsdp", None),
         P(None, None, "fsdp"),
     )
+    body = on_device if dict(mesh.shape) == {"fsdp": 8, "dp": 4} else on_device_any
     return jax.shard_map(
-        on_device, mesh=mesh, in_specs=in_specs, out_specs=out_specs, check_vma=False
-    )
+        body, mesh=mesh, in_specs=in_specs, out_specs=out_specs, check_vma=False
+    )

time: 1020 us -> 980 us (0.961)
  Pallas kernels: 0 us -> 190 us
  waiting for transfers between devices: 687 us -> 503 us
  matrix products: 169 us -> 93.4 us
  local copies, waits for them, and re-layouts: 68.4 us -> 99.5 us
  blocking collectives: 31.8 us -> 12.2 us
  other arithmetic: 41.6 us -> 55.9 us
    pallas_call x0 -> x1, Pallas kernels: none -> 190 us  [forward(): pl.pallas_call(forward_kernel, name='forward', out_shape=out_shape, in_sp...]
    all_gather x8 -> x0, waiting for transfers between devices: 174 us -> none  [the longest x2 75.7 us: on_device(): lax.all_gather(parts_now[2], 'fsdp', axis=0, tiled=True)]
    reduce_scatter x2 -> x0, waiting for transfers between devices: 88 us -> none  [on_device(): lax.psum_scatter(weight_grads[0].astype(jnp.bfloat16), 'fsdp', scatter_di...]
    reduce_scatter x2, waiting for transfers between devices: 0.04 us -> 79.3 us  [on_device(): lax.psum_scatter(weight_grads[1].astype(jnp.bfloat16), 'fsdp', scatter_di...]
    dot_general x10 -> x0, matrix products: 70.2 us -> none  [the longest x2 40.9 us: layer_forward(): jnp.dot(first_low, in_used, preferred_element_type=jnp.float32)]
    unnamed x240 -> x248, local copies, waits for them, and re-layouts: 27.3 us -> 52 us
    all_gather x2 -> x0, blocking collectives: 19.6 us -> none  [on_device(): lax.all_gather(parts_now[4], 'fsdp', axis=1, tiled=True)]
    convert_element_type x10 -> x0, local copies, waits for them, and re-layouts: 16.7 us -> none  [the longest x2 7.25 us: layer_forward(): (jnp.dot(hidden_low, qkv_used, preferred_element_type=jnp.float32) + bias...]
  transfers between devices with their start and end apart: 19 -> 11, of which waited for: 17 -> 10; matrix products, arithmetic and copies ran while one was open for 18% -> 11% of each run, Pallas kernels for 0% -> 0%
where the time goes in v1:
time: 980 us; the launch traced here: 970 us
  waiting for transfers between devices  503 us (51%)
  Pallas kernels  190 us (19%)
  local copies, waits for them, and re-layouts  99.5 us (10%)
  matrix products  93.4 us (10%)
  other arithmetic  55.9 us (6%)
  between operations  15.3 us (2%)
  blocking collectives  12.2 us (1%)
    pallas_call x1, Pallas kernels, forward(): pl.pallas_call(forward_kernel, name='forward', out_shape=out_shape, in_sp...  190 us
    psum x1, waiting for transfers between devices, on_device(): lax.psum(shards[0].astype(jnp.bfloat16), 'dp').astype(jnp.float32)  134 us
    reduce_scatter x2, waiting for transfers between devices, on_device(): lax.psum_scatter(weight_grads[3].astype(jnp.bfloat16), 'fsdp', scatter_di...  115 us
    reduce_scatter x2, waiting for transfers between devices, on_device(): lax.psum_scatter(weight_grads[2].astype(jnp.bfloat16), 'fsdp', scatter_di...  115 us
    reduce_scatter x2, waiting for transfers between devices, on_device(): lax.psum_scatter(weight_grads[1].astype(jnp.bfloat16), 'fsdp', scatter_di...  79.3 us
    unnamed x15, waiting for transfers between devices  58.9 us
    unnamed x248, local copies, waits for them, and re-layouts  52 us
    another operation x17, other arithmetic, adam_step(): return jnp.stack([gradient, updated, second_moment])  24.1 us
  transfers between devices with their start and end apart: 11, of which 10 were waited for; matrix products, arithmetic and copies ran while one was open for 11% of the time, Pallas kernels for 0%

profile of v1, /device:TPU:0, one launch (start us, length us, event | category | flops | bytes accessed | tf_op | source)
XLA Modules:
  0.0 969.7 jit_solution(962123422483706158)
XLA Ops:
  15.4 190.3 %forward.1 = (bf16[512,768]{1,0:T(8,128)(2,1)}, bf16[2,768,2304]{2,1,0:T(8,128)(2,1)}, bf16[2,768,768]{2,1,0:T(8,128)(2,1)}, bf16[2,768,3072]{2,1,0:T(8,128)(2,1...) custom-call(bf16[512,768]{1,0:T(8,128)(2,1)} %tok_ref.1, ...), custom_call_target="tpu_custom_call" | custom-call | tf_op jit(solution)/shard_map/forward/pallas_call | solution.py:425
  212.8 7.4 fusion.235
  220.2 4.6 fusion.63
  236.8 4.6 copy.120
  241.3 4.6 reshape_squeeze.9
  278.2 6.7 fusion.59
  285.9 8.5 fusion.236
  332.9 6.4 convolution_convert_fusion.2
  339.4 6.5 convolution_convert_fusion.3
  347.3 6.8 convolution_convert_fusion
  355.5 6.7 convolution_convert_fusion.1
  368.4 9.5 reduce-scatter.31.cloned.1.call-done
  379.9 38.5 %reduce-scatter.21.cloned.1.call-done = bf16[96,768]{1,0:T(8,128)(2,1)} async-done(((bf16[768,768]{1,0:T(8,128)(2,1)}), bf16[96,768]{1,0:T(8,128)(2,1)}) %reduce-scatter.21.cloned.1.call-update) | async-done | bytes 147472 | tf_op jit(solution)/shard_map/reduce_scatter | solution.py:789
  418.4 40.8 %reduce-scatter.19.cloned.1.call-done = bf16[96,768]{1,0:T(8,128)(2,1)} async-done(((bf16[768,768]{1,0:T(8,128)(2,1)}), bf16[96,768]{1,0:T(8,128)(2,1)}) %reduce-scatter.19.cloned.1.call-update) | async-done | bytes 147472 | tf_op jit(solution)/shard_map/reduce_scatter | solution.py:789
  459.2 57.2 %reduce-scatter.25.cloned.1.call-done = bf16[96,3072]{1,0:T(8,128)(2,1)} async-done(((bf16[768,3072]{1,0:T(8,128)(2,1)}), bf16[96,3072]{1,0:T(8,128)(2,1)}) %reduce-scatter.25.cloned.1.call-update) | async-done | bytes 589840 | tf_op jit(solution)/shard_map/reduce_scatter | solution.py:792
  516.4 57.6 %reduce-scatter.23.cloned.1.call-done = bf16[96,3072]{1,0:T(8,128)(2,1)} async-done(((bf16[768,3072]{1,0:T(8,128)(2,1)}), bf16[96,3072]{1,0:T(8,128)(2,1)}) %reduce-scatter.23.cloned.1.call-update) | async-done | bytes 589840 | tf_op jit(solution)/shard_map/reduce_scatter | solution.py:792
  574.0 57.4 %reduce-scatter.29.cloned.1.call-done = bf16[384,768]{1,0:T(8,128)(2,1)} async-done(((bf16[3072,768]{1,0:T(8,128)(2,1)}), bf16[384,768]{1,0:T(8,128)(2,1)}) %reduce-scatter.29.cloned.1.call-update) | async-done | bytes 589840 | tf_op jit(solution)/shard_map/reduce_scatter | solution.py:795
  631.4 57.7 %reduce-scatter.27.cloned.1.call-done = bf16[384,768]{1,0:T(8,128)(2,1)} async-done(((bf16[3072,768]{1,0:T(8,128)(2,1)}), bf16[384,768]{1,0:T(8,128)(2,1)}) %reduce-scatter.27.cloned.1.call-update) | async-done | bytes 589840 | tf_op jit(solution)/shard_map/reduce_scatter | solution.py:795
  707.7 5.9 fusion.83
  713.6 12.7 %reduce-scatter.37.cloned.1.call-done = bf16[96,12]{1,0:T(8,128)(2,1)} async-done(((bf16[768,12]{1,0:T(8,128)(2,1)}), bf16[96,12]{1,0:T(8,128)(2,1)}) %reduce-scatter.37.cloned.1.call-update) | async-done | bytes 2320
  727.1 36.5 %reduce-scatter.35.cloned.1.call-done = bf16[96,12]{1,0:T(8,128)(2,1)} async-done(((bf16[768,12]{1,0:T(8,128)(2,1)}), bf16[96,12]{1,0:T(8,128)(2,1)}) %reduce-scatter.35.cloned.1.call-update) | async-done | bytes 2320
  764.4 12.2 %all-reduce.1 = (bf16[12,96]{1,0:T(8,128)(2,1)S(1)}, bf16[12,96]{1,0:T(8,128)(2,1)S(1)}) all-reduce(bf16[12,96]{1,0:T(8,128)(2,1)S(1)} %copy.163, bf16[12,96]{1,0:T(8,128)(2,1)S(1)} %copy.161), channel_id=1, replica_groups=mesh['fsdp'=8,'dp'=4] {'dp'}, use_global_device_ids=true, to_apply=%region_49.50 | all-reduce | flops 2304 | bytes 9216 | tf_op jit(solution)/shard_map/psum | solution.py:807
  778.6 134.4 %all-reduce.5.cloned.1.call-done = (bf16[96,2304]{0,1:T(8,128)(2,1)}, bf16[96,2304]{0,1:T(8,128)(2,1)}, bf16[96,768]{1,0:T(8,128)(2,1)}, bf16[96,768]{1,0:T(8,12...) async-done(((bf16[96,2304]{0,1:T(8,128)(2,1)}, bf16[96,2304]{0,1:T(8,128)(2,1)}, ...) | async-done | bytes 3538960 | tf_op jit(solution)/shard_map/psum | solution.py:803
  933.5 5.8 fusion.117
  (393 shorter events, 175.2 us)
Async XLA Ops:
  7.2 359.1 %reduce-scatter.33.cloned.1.call-start = ((), (), s32[]{:S(2)}) async-start(), calls=%async_computation.17 | async-start | bytes 3981312
  211.7 8.4 slice-start.4
  212.8 7.4 copy-start.60
  212.8 7.4 copy-start.43
  212.8 7.4 slice-start.5
  212.8 7.4 slice-start.6
  236.8 10.9 %copy-start.39 = (bf16[4,128,1,12,64]{1,0,4,3,2:T(4,128)(2,1)}, bf16[4,128,1,12,64]{1,0,4,3,2:T(4,128)(2,1)S(1)}, u32[]{:S(2)}) copy-start(bf16[4,128,1,12,64]{1,0,4,3,2:T(4,128)(2,1)S(1)} %get-tuple-element.164) | copy-start | bytes 2359300
  277.5 100.3 %reduce-scatter.31.cloned.1.call-start = ((), (), s32[]{:S(2)}) async-start(), calls=%async_computation.16 | async-start | bytes 3981312
  278.2 6.7 copy-start.82
  284.9 9.5 slice-start.7
  285.9 8.5 copy-start.62
  285.9 8.5 copy-start.45
  285.9 8.5 slice-start.8
  285.9 8.5 slice-start.9
  325.2 93.2 %reduce-scatter.21.cloned.1.call-start = ((), (), s32[]{:S(2)}) async-start(), calls=%async_computation.11 | async-start | bytes 1327104 | tf_op jit(solution)/shard_map/reduce_scatter | solution.py:789
  329.7 129.5 %reduce-scatter.19.cloned.1.call-start = ((), (), s32[]{:S(2)}) async-start(), calls=%async_computation.10 | async-start | bytes 1327104 | tf_op jit(solution)/shard_map/reduce_scatter | solution.py:789
  332.9 183.6 %reduce-scatter.25.cloned.1.call-start = ((), (), s32[]{:S(2)}) async-start(), calls=%async_computation.13 | async-start | bytes 5308416 | tf_op jit(solution)/shard_map/reduce_scatter | solution.py:792
  339.3 234.7 %reduce-scatter.23.cloned.1.call-start = ((), (), s32[]{:S(2)}) async-start(), calls=%async_computation.12 | async-start | bytes 5308416 | tf_op jit(solution)/shard_map/reduce_scatter | solution.py:792
  345.9 285.5 %reduce-scatter.29.cloned.1.call-start = ((), (), s32[]{:S(2)}) async-start(), calls=%async_computation.15 | async-start | bytes 5308416 | tf_op jit(solution)/shard_map/reduce_scatter | solution.py:795
  354.1 335.0 %reduce-scatter.27.cloned.1.call-start = ((), (), s32[]{:S(2)}) async-start(), calls=%async_computation.14 | async-start | bytes 5308416 | tf_op jit(solution)/shard_map/reduce_scatter | solution.py:795
  362.3 364.0 %reduce-scatter.37.cloned.1.call-start = ((), (), s32[]{:S(2)}) async-start(), calls=%async_computation.19 | async-start | bytes 221184
  364.8 398.8 %reduce-scatter.35.cloned.1.call-start = ((), (), s32[]{:S(2)}) async-start(), calls=%async_computation.18 | async-start | bytes 221184
  366.3 546.7 %all-reduce.5.cloned.1.call-start = ((), (), s32[]{:S(2)}) async-start(), calls=%async_computation.20 | async-start | bytes 7667712 | tf_op jit(solution)/shard_map/psum | solution.py:803
  928.7 10.6 %slice-start = ((s8[4718592]{0:T(1024)(128)(4,1)}), s8[524288]{0:T(1024)(128)(4,1)S(1)}, s32[]{:S(2)}) async-start(s8[4718592]{0:T(1024)(128)(4,1)} %bitcast.432), calls=%async_computation.21 | async-start | bytes 1048576
  (101 other events, 265.2 us)
Sparse Core Ops, SparseCore 0:
  277.6 48.5 reduce-scatter.32
  329.8 48.0 reduce-scatter.30
  381.7 36.7 reduce-scatter.20
  422.4 36.7 reduce-scatter.18
  462.5 53.8 reduce-scatter.24
  520.1 53.8 reduce-scatter.22
  577.4 53.8 reduce-scatter.28
  635.2 53.8 reduce-scatter.26
  692.7 33.5 reduce-scatter.36
  730.0 33.5 reduce-scatter.34
  767.2 145.7 all-reduce.4
